TPU v7x, 1024 devices: a whole 4x4x32 slice. The times are simulated.
1024 devices in a mesh: dp: 16 (over x_lo, y, core), seq: 64 (over x_hi, z).
Axes of the slice: x: 4 (x_hi: 2, x_lo: 2; x = x_hi * 2 + x_lo), y: 4, z: 32, core: 2. Of those that a mesh axis runs over, the one named last changes fastest.
Arguments:
- inputs: bfloat16 [16, 12288, 768], P('dp', 'seq'), may hold values from -6 to 6
- cotangent: bfloat16 [16, 12288, 768], P('dp', 'seq'), may hold values from -16 to 16
- dilated_kernel_weight: bfloat16 [768, 3, 384], P('dp'), may hold values from -0.125 to 0.125
- point_weight: bfloat16 [384, 768], P('dp'), may hold values from -0.3125 to 0.3125
Outputs:
- grad_input: bfloat16 [16, 12288, 768], P('dp', 'seq')
- kernel_weight_gradient: float32 [768, 3, 384], P('dp')
- pointwise_weight_gradient: float32 [384, 768], P('dp')
All inputs are finite; a program needn't handle non-finite values.
Results may differ from a plain program's by a relative error of at most 0.0054.
Values may be sent and summed in bfloat16 or wider, within the bound.
No kernel may reach another device: no remote copies, remote signals or barrier semaphores. Data moves between devices by JAX's collectives and lax.ppermute only.
A program may use at most 32 MiB of HBM per device.

v0:
```python
import jax
import jax.numpy as jnp
from jax import lax
from jax.sharding import PartitionSpec as P

DILATION_SPAN = 32


def extended(x, sides, width):
    for axis, dim in sides:
        size, length = (lax.axis_size(axis), x.shape[dim])
        up = [(i, (i + 1) % size) for i in range(size - 1)]
        down = [(j, i) for i, j in up]
        last = lax.slice_in_dim(x, length - width, length, axis=dim)
        initial = lax.slice_in_dim(x, 0, width, axis=dim)
        before = lax.ppermute(last, axis, up)
        after = lax.ppermute(initial, axis, down)
        x = jnp.concatenate([before, x, after], axis=dim)
    return x


def gelu_apply(values):
    return jax.nn.gelu(values, approximate=True)


def rms_normed(values):
    return values * lax.rsqrt(jnp.mean(values * values, axis=-1, keepdims=True) + 1e-06)


def conv_forward(padded_activation, weight_full, output_length):
    return sum(
        (
            jnp.einsum(
                "amv,vb->amb",
                padded_activation[
                    :,
                    kernel_tap_index * DILATION_SPAN : kernel_tap_index * DILATION_SPAN
                    + output_length,
                ],
                weight_full[:, kernel_tap_index, :],
                preferred_element_type=jnp.float32,
            )
            for kernel_tap_index in range(3)
        )
    )


def conv_weight_grad(padded_activation, delta_rows, input_length):
    return jnp.stack(
        [
            jnp.einsum(
                "hyr,hyk->rk",
                padded_activation[
                    :,
                    kernel_tap_index * DILATION_SPAN : kernel_tap_index * DILATION_SPAN
                    + input_length,
                ],
                delta_rows,
                preferred_element_type=jnp.float32,
            )
            for kernel_tap_index in range(3)
        ],
        axis=1,
    )


def conv_backward(padded_delta, weight_full, input_length):
    return sum(
        (
            jnp.einsum(
                "mfi,xi->mfx",
                padded_delta[
                    :,
                    (2 - kernel_tap_index) * DILATION_SPAN : (2 - kernel_tap_index) * DILATION_SPAN
                    + input_length,
                ],
                weight_full[:, kernel_tap_index, :],
                preferred_element_type=jnp.float32,
            )
            for kernel_tap_index in range(3)
        )
    )


def per_device(inputs, cotangent, dilated_kernel_weight, point_weight):
    conv_full, pointwise_full_weight = (
        lax.all_gather(dilated_kernel_weight, "dp", axis=0, tiled=True),
        lax.all_gather(point_weight, "dp", axis=0, tiled=True),
    )
    input_length = inputs.shape[1]
    normal, pull_norm = jax.vjp(rms_normed, inputs.astype(jnp.float32))
    activated_hidden, pull_act = jax.vjp(gelu_apply, normal)
    padded_activation = extended(
        activated_hidden.astype(jnp.bfloat16), (("seq", 1),), DILATION_SPAN
    )
    preactivation = conv_forward(padded_activation, conv_full, input_length)
    hidden, pull_hidden = jax.vjp(gelu_apply, preactivation)
    hidden_halfprec = hidden.astype(jnp.bfloat16)
    pointwise_weight_gradient = jnp.einsum(
        "xth,xtr->hr", hidden_halfprec, cotangent, preferred_element_type=jnp.float32
    )
    upstream_gradient = jnp.einsum(
        "pqy,oy->pqo", cotangent, pointwise_full_weight, preferred_element_type=jnp.float32
    )
    delta_rows = pull_hidden(upstream_gradient)[0].astype(jnp.bfloat16)
    kernel_weight_gradient = conv_weight_grad(padded_activation, delta_rows, input_length)
    padded_delta = extended(delta_rows, (("seq", 1),), DILATION_SPAN)
    activation_gradient = conv_backward(padded_delta, conv_full, input_length)
    grad_normal = pull_act(activation_gradient)[0]
    grad_inner = pull_norm(grad_normal)[0]
    grad_input = (cotangent.astype(jnp.float32) + grad_inner).astype(jnp.bfloat16)
    owned_conv, owned_point = (
        lax.psum_scatter(kernel_weight_gradient, "dp", scatter_dimension=0, tiled=True),
        lax.psum_scatter(pointwise_weight_gradient, "dp", scatter_dimension=0, tiled=True),
    )
    owned_conv, owned_point = lax.psum((owned_conv, owned_point), "seq")
    return (grad_input, owned_conv, owned_point)


def solution(mesh):
    return jax.shard_map(
        per_device,
        mesh=mesh,
        in_specs=(P("dp", "seq", None), P("dp", "seq", None), P("dp", None, None), P("dp", None)),
        out_specs=(P("dp", "seq", None), P("dp", None, None), P("dp", None)),
        check_vma=False,
    )
```

profile of v0, /device:TPU:2, one launch (start us, length us, event | category | flops | bytes accessed | tf_op | source)
XLA Modules:
  0.0 804.5 jit_solution(12002192726019277121)
XLA Ops:
  7.2 0.7 all-gather.2.cloned.1.call-update
  7.9 1.1 fusion.19
  9.1 1.3 fusion.16
  10.3 3.8 collective-permute-start
  14.2 1.3 collective-permute-start.1
  15.5 54.5 %all-gather.2.cloned.1.call-done = bf16[768,3,384]{2,0,1:T(8,128)(2,1)} async-done(((bf16[48,3,384]{2,0,1:T(8,128)(2,1)}), bf16[768,3,384]{2,0,1:T(8,128)(2,1)}) %all-gather.2.cloned.1.call-update) | async-done | bytes 1769488 | tf_op jit(solution)/shard_map/all_gather | solution.py:87
  70.0 1.5 fusion.22
  71.5 1.4 fusion.24
  73.3 1.4 fusion.36
  74.8 19.6 %all_gather.6 = bf16[384,768]{1,0:T(8,128)(2,1)S(1)} all-gather(bf16[24,768]{1,0:T(8,128)(2,1)S(1)} %copy-done.3), channel_id=1, replica_groups=mesh['dp'=16,'seq'=64] {'dp'}, dimensions={0}, use_global_device_ids=true | all-gather | bytes 626688 | tf_op jit(solution)/shard_map/all_gather | solution.py:88
  94.4 0.4 fusion.31
  94.8 0.4 convolution_bitcast_fusion
  95.2 0.4 convolution_bitcast_fusion.2
  96.0 2.0 pad_maximum_fusion
  98.1 1.4 collective-permute-start.2
  99.5 4.5 collective-permute-start.3
  104.5 1.1 collective-permute-done.3
  106.0 0.8 fusion.20
  106.8 47.3 %reduce-scatter.5.cloned.1.call-done = f32[24,768]{1,0:T(8,128)} async-done(((f32[384,768]{1,0:T(8,128)}), f32[24,768]{1,0:T(8,128)}) %reduce-scatter.5.cloned.1.call-update) | async-done | bytes 73744 | tf_op jit(solution)/shard_map/reduce_scatter | solution.py:114
  154.1 86.4 %reduce-scatter.3.cloned.1.call-done = f32[48,3,384]{2,0,1:T(8,128)} async-done(((f32[768,3,384]{2,0,1:T(8,128)}), f32[48,3,384]{2,0,1:T(8,128)}) %reduce-scatter.3.cloned.1.call-update) | async-done | bytes 221200 | tf_op jit(solution)/shard_map/reduce_scatter | solution.py:113
  240.5 0.9 fusion.12
  241.4 553.4 %all-reduce.3.cloned.1.call-done = (f32[48,3,384]{2,0,1:T(8,128)}, f32[24,768]{1,0:T(8,128)}) async-done(((f32[48,3,384]{2,0,1:T(8,128)}, f32[24,768]{1,0:T(8,128)}), (f32[48,3,384]{2,0,1:T(8,128)}, f32[24,768]{1,0:T(8,128)})) %all-reduce.3.cloned.1.call-update) | async-done | bytes 294928 | tf_op jit(solution)/shard_map/psum | solution.py:116
  794.8 1.6 copy.9
  796.4 1.5 copy.10
  (26 shorter events, 1.7 us)
Async XLA Ops:
  7.2 62.8 %all-gather.2.cloned.1.call-start = ((), (), s32[]{:S(2)}) async-start(), calls=%async_computation.2 | async-start | bytes 1880064 | tf_op jit(solution)/shard_map/all_gather | solution.py:87
  7.9 146.2 %reduce-scatter.5.cloned.1.call-start = ((), (), s32[]{:S(2)}) async-start(), calls=%async_computation.4 | async-start | bytes 1253376 | tf_op jit(solution)/shard_map/reduce_scatter | solution.py:114
  10.3 62.6 %collective-permute-start = (bf16[1,32,768]{2,1,0:T(8,128)(2,1)S(1)}, bf16[1,32,768]{2,1,0:T(8,128)(2,1)S(1)}, u32[]{:S(2)}, u32[]{:S(2)}) collective-permute-start(bf16[1,32,768]{2,1,0:T(8,128)(2,1)S(1)} %get-tuple-element.5), channel_id=1, source_target_pairs={{0,1},{1,2},{2,3},{3,4},{4,5},{5,6},{6,7},{7,8},{8,9},{9,10},{10,1... | collective-permute-start | bytes 147464 | tf_op jit(solution)/shard_map/ppermute | solution.py:16
  14.2 57.3 %collective-permute-start.1 = (bf16[1,32,768]{2,1,0:T(8,128)(2,1)S(1)}, bf16[1,32,768]{2,1,0:T(8,128)(2,1)S(1)}, u32[]{:S(2)}, u32[]{:S(2)}) collective-permute-start(bf16[1,32,768]{2,1,0:T(8,128)(2,1)S(1)} %get-tuple-element.6), channel_id=1, source_target_pairs={{1,0},{2,1},{3,2},{4,3},{5,4},{6,5},{7,6},{8,7},{9,8},{10,9},{11,1... | collective-permute-start | bytes 147464 | tf_op jit(solution)/shard_map/ppermute | solution.py:17
  70.0 3.0 copy-start
  71.5 1.8 copy-start.2
  73.3 1.5 copy-start.3
  74.8 165.7 %reduce-scatter.3.cloned.1.call-start = ((), (), s32[]{:S(2)}) async-start(), calls=%async_computation.3 | async-start | bytes 3760128 | tf_op jit(solution)/shard_map/reduce_scatter | solution.py:113
  98.0 7.9 copy-start.1
  98.0 696.7 %all-reduce.3.cloned.1.call-start = ((), (), s32[]{:S(2)}) async-start(), calls=%async_computation.5 | async-start | bytes 589824 | tf_op jit(solution)/shard_map/psum | solution.py:116
  98.1 7.9 collective-permute-start.2
  99.5 6.1 collective-permute-start.3
Sparse Core Ops, SparseCore 0:
  10.6 59.2 all-gather.1
  74.9 79.1 reduce-scatter.4
  157.5 82.8 reduce-scatter.2
  243.8 550.8 all-reduce.2
where the time goes:
time: 805 us; the launch traced here: 804 us
  waiting for transfers between devices  743 us (92%)
  blocking collectives  19.6 us (2%)
  between operations  13.9 us (2%)
  starting transfers between devices  11.2 us (1%)
    psum x1, waiting for transfers between devices, per_device(): owned_conv, owned_point = lax.psum((owned_conv, owned_point), 'seq')  553 us
    reduce_scatter x1, waiting for transfers between devices, per_device(): lax.psum_scatter(kernel_weight_gradient, 'dp', scatter_dimension=0, tiled...  86.4 us
    all_gather x1, waiting for transfers between devices, per_device(): lax.all_gather(dilated_kernel_weight, 'dp', axis=0, tiled=True)  54.5 us
    reduce_scatter x1, waiting for transfers between devices, per_device(): lax.psum_scatter(pointwise_weight_gradient, 'dp', scatter_dimension=0, ti...  47.3 us
    all_gather x1, blocking collectives, per_device(): lax.all_gather(point_weight, 'dp', axis=0, tiled=True)  19.6 us
  transfers between devices with their start and end apart: 8, of which 5 were waited for; matrix products, arithmetic and copies ran while one was open for 1% of the time, Pallas kernels for 0%

commit v1 on v0

v1 whole, which is shorter than its diff:
```python
import jax
import jax.numpy as jnp
from jax import lax
from jax.experimental import pallas as pl
from jax.experimental.pallas import tpu as pltpu
from jax.sharding import Mesh
from jax.sharding import PartitionSpec as P


SPAN = 32
EPS = 1e-06
ALPHA = 0.7978845608028654
BETA = 0.044715
ZL = 2
DP = ("xl", "y", "c")
SEQ = ("xh", "zh", "zl")
PAIR = [(0, 1), (1, 0)]
BF16, F32 = jnp.bfloat16, jnp.float32


def dot(a, b, ca, cb):
    return lax.dot_general(a, b, (((ca,), (cb,)), ((), ())), preferred_element_type=F32)


def gelu_value(v):
    return 0.5 * v * (1.0 + jnp.tanh(ALPHA * (v + BETA * (v * v * v))))


def gelu_both(v):
    t = jnp.tanh(ALPHA * (v + BETA * (v * v * v)))
    half = 0.5 * (1.0 + t)
    slope = half + 0.5 * v * (1.0 - t * t) * (ALPHA * (1.0 + 3.0 * BETA * (v * v)))
    return v * half, slope


def inverse_rms(x):
    return lax.rsqrt(jnp.mean(x * x, axis=-1, keepdims=True) + EPS)


def pack_body(wk, wp, xa, xb, ca, cb, copies, up, down):
    taps, rows, ci = wk.shape
    w = [wk[k] for k in range(taps)]
    p = wp[...].astype(F32)
    p = jnp.concatenate([p[:, :ci], p[:, ci:]], axis=0).astype(BF16)
    for i in range(copies.shape[0]):
        for k in range(taps):
            copies[i, k * rows : (k + 1) * rows] = w[k]
        copies[i, taps * rows :] = p
    up[: 2 * SPAN] = xb[...]
    up[2 * SPAN :] = cb[...]
    down[: 2 * SPAN] = xa[...]
    down[2 * SPAN :] = ca[...]


def act_body(x, cot, before, after, act, wide):
    n, h = x.shape[0], 2 * SPAN

    def part(v):
        v = v.astype(F32)
        return gelu_value(v * inverse_rms(v)).astype(BF16)

    act[:h] = part(before[:h])
    act[h : h + n] = part(x[...])
    act[h + n :] = part(after[:h])
    wide[:SPAN] = before[h:]
    wide[SPAN : SPAN + n] = cot[...]
    wide[SPAN + n :] = after[h:]


def main_body(c_ref, near, far, act, wide, delta, wk, mine, send, wp_s, dk_s, dp_s):
    c = c_ref[0]
    groups, _, ci = near.shape
    taps, channels, _ = wk.shape
    rows, prow = channels // (2 * groups), ci // (2 * groups)
    m = wide.shape[0]
    n = m - 2 * SPAN
    for ref, core in ((near, c), (far, 1 - c)):
        for i in range(groups):
            d = 2 * i + core
            for k in range(taps):
                wk[k, pl.ds(pl.multiple_of(d * rows, rows), rows)] = ref[i, k * rows : (k + 1) * rows]
            p = ref[i, taps * rows :].astype(F32)
            at = pl.ds(pl.multiple_of(d * prow, prow), prow)
            wp_s[at, :ci] = p[:prow]
            wp_s[at, ci:] = p[prow:]
    preact = dot(act[:m], wk[0], 1, 0)
    for k in range(1, taps):
        preact = preact + dot(act[k * SPAN : k * SPAN + m], wk[k], 1, 0)
    hidden, slope = gelu_both(preact)
    upstream = dot(wide[...], wp_s[...].astype(BF16), 1, 1)
    deltas = (upstream * slope).astype(BF16)
    delta[...] = deltas
    dp_s[...] = dot(hidden[SPAN : SPAN + n].astype(BF16), wide[SPAN : SPAN + n], 0, 0)
    inner = deltas[SPAN : SPAN + n]
    for k in range(taps):
        dk_s[k] = dot(act[(k + 1) * SPAN : (k + 1) * SPAN + n], inner, 0, 0)
    for ref, core in ((mine, c), (send, 1 - c)):
        for i in range(groups):
            d = 2 * i + core
            for k in range(taps):
                v = dk_s[k, pl.ds(pl.multiple_of(d * rows, rows), rows)]
                ref[i, k * rows : (k + 1) * rows] = v.astype(ref.dtype)
            at = pl.ds(pl.multiple_of(d * prow, prow), prow)
            v = jnp.concatenate([dp_s[at, :ci], dp_s[at, ci:]], axis=0)
            ref[i, taps * rows :] = v.astype(ref.dtype)


def input_body(delta, wk, x, cot, out):
    taps, n = wk.shape[0], x.shape[0]
    grad = dot(delta[(taps - 1) * SPAN : (taps - 1) * SPAN + n], wk[0], 1, 1)
    for k in range(1, taps):
        at = (taps - 1 - k) * SPAN
        grad = grad + dot(delta[at : at + n], wk[k], 1, 1)
    v = x[...].astype(F32)
    r = inverse_rms(v)
    _, slope = gelu_both(v * r)
    g = grad * slope
    inner = r * g - v * (r * r * r * jnp.mean(v * g, axis=-1, keepdims=True))
    out[...] = (cot[...].astype(F32) + inner).astype(BF16)


def sds(shape, dtype):
    return jax.ShapeDtypeStruct(shape, dtype)


def in_hbm(a):
    return pltpu.with_memory_space_constraint(a, pltpu.HBM)


def limit(mib):
    return pltpu.CompilerParams(vmem_limit_bytes=mib << 20)


def copies_to(x, axis):
    n = lax.axis_size(axis)
    y = jnp.broadcast_to(x[None], (n,) + x.shape).reshape((n * x.shape[0],) + x.shape[1:])
    return lax.all_to_all(y, axis, 0, 0, tiled=True)


def exchanged_sum(x, axis):
    n = lax.axis_size(axis)
    y = lax.all_to_all(x, axis, 0, 0, tiled=True)
    return jnp.sum(y.reshape((n, x.shape[0] // n) + x.shape[1:]).astype(F32), axis=0)


def per_device(inputs, cotangent, dilated_kernel_weight, point_weight):
    x, cot = inputs[0], cotangent[0]
    n, C = x.shape
    rows, taps, CI = dilated_kernel_weight.shape
    prow = point_weight.shape[0]
    total = taps * rows + 2 * prow
    groups = lax.axis_size("xl") * lax.axis_size("y")
    seq = lax.axis_size(SEQ)
    core = lax.axis_index("c")
    h = 2 * SPAN
    whole = lambda *s: pl.BlockSpec(s, lambda *_: (0,) * len(s))

    last = n // h - 1
    edge = n // SPAN - 1
    copies, up, down = pl.pallas_call(
        pack_body,
        grid=(1,),
        in_specs=[
            whole(taps, rows, CI),
            whole(prow, C),
            pl.BlockSpec((h, C), lambda i: (0, 0)),
            pl.BlockSpec((h, C), lambda i: (last, 0)),
            pl.BlockSpec((SPAN, C), lambda i: (0, 0)),
            pl.BlockSpec((SPAN, C), lambda i: (edge, 0)),
        ],
        out_specs=[whole(groups, total, CI), whole(h + SPAN, C), whole(h + SPAN, C)],
        out_shape=[sds((groups, total, CI), BF16), sds((h + SPAN, C), BF16), sds((h + SPAN, C), BF16)],
        name="pack",
        compiler_params=limit(14),
    )(*map(in_hbm, (jnp.swapaxes(dilated_kernel_weight, 0, 1), point_weight, x, x, cot, cot)))

    after = lax.ppermute(down, SEQ, [(i + 1, i) for i in range(seq - 1)])
    before = lax.ppermute(up, SEQ, [(i, i + 1) for i in range(seq - 1)])
    near = lax.all_to_all(copies.reshape(groups * total, CI), ("xl", "y"), 0, 0, tiled=True)
    far = lax.ppermute(near, "c", PAIR)
    near, far = near.reshape(groups, total, CI), far.reshape(groups, total, CI)

    spec = pl.BlockSpec(memory_space=pltpu.VMEM)
    far = in_hbm(far)
    act, wide = pl.pallas_call(
        act_body,
        in_specs=[spec] * 4,
        out_specs=[spec] * 2,
        out_shape=[sds((n + 2 * h, C), BF16), sds((n + h, C), BF16)],
        name="act",
        compiler_params=limit(14),
    )(x, cot, before, after)
    delta, wk, mine, send = pl.pallas_call(
        main_body,
        in_specs=[pl.BlockSpec(memory_space=pltpu.SMEM)] + [spec] * 4,
        out_specs=[spec] * 4,
        out_shape=[
            sds((n + h, CI), BF16),
            sds((taps, C, CI), BF16),
            sds((groups, total, CI), F32),
            sds((groups, total, CI), BF16),
        ],
        scratch_shapes=[
            pltpu.VMEM((CI, C), F32),
            pltpu.VMEM((taps, C, CI), F32),
            pltpu.VMEM((CI, C), F32),
        ],
        name="main",
        compiler_params=limit(14),
    )(core.reshape(1).astype(jnp.int32), near, far, act, wide)
    got = lax.ppermute(send, "c", PAIR)
    grad_input = pl.pallas_call(input_body, in_specs=[spec] * 4, out_shape=sds((n, C), BF16), name="input_grad", compiler_params=limit(14))(delta, wk, x, cot)

    s = (mine + got.astype(F32)).astype(BF16).reshape(groups * total, CI)
    s = exchanged_sum(s, ("xl", "y", "xh"))
    s = exchanged_sum(s, "zl")
    s = jnp.sum(lax.all_gather(s.astype(BF16), "zh", axis=0).astype(F32), axis=0)
    s = copies_to(s, ("xh", "zl"))
    owned_conv = jnp.swapaxes(s[: taps * rows].reshape(taps, rows, CI), 0, 1)
    q = taps * rows
    owned_point = jnp.concatenate([s[q : q + prow], s[q + prow :]], axis=1)
    return (grad_input[None], owned_conv, owned_point)


def solution(mesh):
    fine = Mesh(mesh.devices.reshape(2, 4, 2, 2, 32 // ZL, ZL), DP + SEQ)
    return jax.shard_map(
        per_device,
        mesh=fine,
        in_specs=(P(DP, SEQ, None), P(DP, SEQ, None), P(DP, None, None), P(DP, None)),
        out_specs=(P(DP, SEQ, None), P(DP, None, None), P(DP, None)),
        check_vma=False,
    )
```

time: 805 us -> 143 us (0.18)
  the two profiles are of different devices: /device:TPU:2 before, /device:TPU:32 now
where the time goes in v1:
time: 143 us
  blocking collectives  103 us (72%)
  starting transfers between devices  17.1 us (12%)
  waiting for transfers between devices  11.1 us (8%)
  Pallas kernels  6.94 us (5%)
  local copies, waits for them, and re-layouts  3.13 us (2%)
    all_to_all x2, blocking collectives, exchanged_sum(): y = lax.all_to_all(x, axis, 0, 0, tiled=True)  41.1 us
    all_gather x1, blocking collectives, per_device(): lax.all_gather(s.astype(BF16), 'zh', axis=0).astype(F32)  38.8 us
    all_to_all x1, blocking collectives, per_device(): lax.all_to_all(copies.reshape(groups * total, CI), ('xl', 'y'), 0, 0, til...  22.6 us
    all_to_all x1, starting transfers between devices, copies_to(): return lax.all_to_all(y, axis, 0, 0, tiled=True)  5.17 us
    all_to_all x1, waiting for transfers between devices, copies_to(): return lax.all_to_all(y, axis, 0, 0, tiled=True)  4.53 us
    ppermute x1, starting transfers between devices, per_device(): after = lax.ppermute(down, SEQ, [(i + 1, i) for i in range(seq - 1)])  4.29 us
    ppermute x1, starting transfers between devices, per_device(): before = lax.ppermute(up, SEQ, [(i, i + 1) for i in range(seq - 1)])  3.83 us
    pallas_call x1, Pallas kernels, per_device(): pl.pallas_call(main_body, in_specs=[pl.BlockSpec(memory_space=pltpu.SMEM)...  3.55 us
  transfers between devices with their start and end apart: 5, of which 4 were waited for; matrix products, arithmetic and copies ran while one was open for 0% of the time, Pallas kernels for 2%

profile of v1, /device:TPU:32, one launch (start us, length us, event | category | flops | bytes accessed | tf_op | source)
XLA Modules:
  0.0 142.7 jit_solution(9052300116159017490)
XLA Ops:
  0.6 1.1 pack.1
  1.8 22.6 %all_to_all.36.near = bf16[8,192,384]{2,1,0:T(8,128)(2,1)S(1)} all-to-all(bf16[8,192,384]{2,1,0:T(8,128)(2,1)S(1)} %get-tuple-element.12), channel_id=1, replica_groups=mesh['xl'=2,'y'=4,'c'=2,'xh'=2,'zh'=16,'zl'=2] {'xl','y'}, dimensions={0} | all-to-all | bytes 2359296 | tf_op jit(solution)/shard_map/all_to_all | solution.py:179
  24.4 1.9 %collective-permute-start = (bf16[1536,384]{1,0:T(8,128)(2,1)S(1)}, bf16[1536,384]{1,0:T(8,128)(2,1)S(1)}, u32[]{:S(2)}, u32[]{:S(2)}) collective-permute-start(bf16[1536,384]{1,0:T(8,128)(2,1)S(1)} %bitcast.14), channel_id=1, source_target_pairs={{0,64},{64,0},{1,65},{65,1},{2,66},{66,2},{3,67},{67,3},{4,68},{68... | collective-permute-start | bytes 3538952 | tf_op jit(solution)/shard_map/ppermute | solution.py:180
  26.3 3.8 %collective-permute-start.1 = (bf16[96,768]{1,0:T(8,128)(2,1)S(1)}, bf16[96,768]{1,0:T(8,128)(2,1)S(1)}, u32[]{:S(2)}, u32[]{:S(2)}) collective-permute-start(bf16[96,768]{1,0:T(8,128)(2,1)S(1)} %get-tuple-element.13), channel_id=1, source_target_pairs={{0,1},{1,2},{2,3},{3,4},{4,5},{5,6},{6,7},{7,8},{8,9},{9,10},{10,1... | collective-permute-start | bytes 442376 | tf_op jit(solution)/shard_map/ppermute | solution.py:178
  30.1 4.3 %collective-permute-start.2 = (bf16[96,768]{1,0:T(8,128)(2,1)S(1)}, bf16[96,768]{1,0:T(8,128)(2,1)S(1)}, u32[]{:S(2)}, u32[]{:S(2)}) collective-permute-start(bf16[96,768]{1,0:T(8,128)(2,1)S(1)} %get-tuple-element.14), channel_id=1, source_target_pairs={{1,0},{2,1},{3,2},{4,3},{5,4},{6,5},{7,6},{8,7},{9,8},{10,9},{11,1... | collective-permute-start | bytes 442376 | tf_op jit(solution)/shard_map/ppermute | solution.py:177
  34.4 2.6 %collective-permute-done.1.before = bf16[96,768]{1,0:T(8,128)(2,1)S(1)} collective-permute-done((bf16[96,768]{1,0:T(8,128)(2,1)S(1)}, bf16[96,768]{1,0:T(8,128)(2,1)S(1)}, u32[]{:S(2)}, u32[]{:S(2)}) %collective-permute-start.1) | collective-permute-done | bytes 147488 | tf_op jit(solution)/shard_map/ppermute | solution.py:178
  37.0 1.2 collective-permute-done.2.after
  38.2 0.5 act.1
  38.7 1.0 copy-done.4
  39.7 3.6 %main.1 = (bf16[256,384]{1,0:T(8,128)(2,1)S(1)}, bf16[3,768,384]{2,1,0:T(8,128)(2,1)S(1)}, f32[8,192,384]{2,1,0:T(8,128)S(1)}, bf16[8,192,384]{2,1,0:T(8,128)(2,1)S(1)}) custom-call(s32[1]{0:T(128)} %bitcast.c_ref, bf16[8,192,384]{2,1,0:T(8,128)(2,1)S(1)} %all_to_all.36.near, bf16[8,192,384]{2,1,0:T(8,128)(2,1)} %bitcast.25, ...), custom_call_target="tpu_custom_call" | custom-call | tf_op jit(solution)/shard_map/main/pallas_call | solution.py:193
  43.3 0.7 copy-done.2
  43.9 1.9 %collective-permute-start.3 = (bf16[8,192,384]{2,1,0:T(8,128)(2,1)S(1)}, bf16[8,192,384]{2,1,0:T(8,128)(2,1)S(1)}, u32[]{:S(2)}, u32[]{:S(2)}) collective-permute-start(bf16[8,192,384]{2,1,0:T(8,128)(2,1)S(1)} %get-tuple-element.20), channel_id=1, source_target_pairs={{0,64},{64,0},{1,65},{65,1},{2,66},{66,2},{3,67},{67,3},{4,68},{68... | collective-permute-start | bytes 3538952 | tf_op jit(solution)/shard_map/ppermute | solution.py:211
  45.9 2.8 %collective-permute-done.3 = bf16[8,192,384]{2,1,0:T(8,128)(2,1)S(1)} collective-permute-done((bf16[8,192,384]{2,1,0:T(8,128)(2,1)S(1)}, bf16[8,192,384]{2,1,0:T(8,128)(2,1)S(1)}, u32[]{:S(2)}, u32[]{:S(2)}) %collective-permute-start.3) | collective-permute-done | bytes 1179680 | tf_op jit(solution)/shard_map/ppermute | solution.py:211
  48.7 0.3 add_convert_fusion
  49.0 23.4 %all_to_all.37 = bf16[16,96,384]{2,1,0:T(8,128)(2,1)S(1)} all-to-all(bf16[16,96,384]{2,1,0:T(8,128)(2,1)S(1)} %bitcast.23), channel_id=1, replica_groups=mesh['xl'=2,'y'=4,'c'=2,'xh'=2,'zh'=16,'zl'=2] {'xl','y','xh'}, dimensions={0} | all-to-all | bytes 2359296 | tf_op jit(solution)/shard_map/all_to_all | solution.py:142
  72.4 0.2 convert_reduce_fusion
  72.5 17.7 %all_to_all.38 = f32[2,48,384]{2,1,0:T(8,128)S(1)} all-to-all(f32[2,48,384]{2,1,0:T(8,128)S(1)} %bitcast.27), channel_id=1, replica_groups=mesh['xl'=2,'y'=4,'c'=2,'xh'=2,'zh'=16,'zl'=2] {'zl'}, dimensions={0} | all-to-all | bytes 294912 | tf_op jit(solution)/shard_map/all_to_all | solution.py:142
  90.2 38.8 %all-gather = bf16[768,384]{1,0:T(8,128)(2,1)S(1)} all-gather(bf16[48,384]{1,0:T(8,128)(2,1)S(1)} %reduce_sum.28), channel_id=2, replica_groups=mesh['xl'=2,'y'=4,'c'=2,'xh'=2,'zh'=16,'zl'=2] {'zh'}, dimensions={0}, use_global_device_ids=true | all-gather | bytes 626688 | tf_op jit(solution)/shard_map/all_gather | solution.py:217
  129.2 0.7 broadcast_in_dim.10
  129.9 5.2 %all-to-all-start.3 = ((f32[4,48,384]{2,1,0:T(8,128)}), f32[4,48,384]{2,1,0:T(8,128)S(1)}, u32[]{:S(2)}, u32[]{:S(2)}) async-start(f32[4,48,384]{2,1,0:T(8,128)} %broadcast_in_dim.10), calls=%async_computation.3 | async-start | bytes 589824 | tf_op jit(solution)/shard_map/all_to_all | solution.py:137
  135.1 1.8 %input_grad.1 = bf16[192,768]{1,0:T(8,128)(2,1)} custom-call(bf16[256,384]{1,0:T(8,128)(2,1)S(1)} %copy-done.3, bf16[3,768,384]{2,1,0:T(8,128)(2,1)S(1)} %get-tuple-element.18.wk, bf16[192,768]{1,0:T(8,128)(2,1)S(1)} %bitcast.18, bf16[192,768]{1,0:T(8,128)(2,1)S(1)} %bitcast.22), custom_call_target="tpu_custom_call" | custom-call | tf_op jit(solution)/shard_map/input_grad/pallas_call | solution.py:212
  136.8 4.5 %all-to-all-done.3 = f32[4,48,384]{2,1,0:T(8,128)S(1)} async-done(((f32[4,48,384]{2,1,0:T(8,128)}), f32[4,48,384]{2,1,0:T(8,128)S(1)}, u32[]{:S(2)}, u32[]{:S(2)}) %all-to-all-start.3) | async-done | bytes 294944 | tf_op jit(solution)/shard_map/all_to_all | solution.py:137
  141.4 0.6 pad_maximum_fusion
  142.0 0.7 slice_bitcast_fusion
  (12 shorter events, 0.1 us)
Async XLA Ops:
  1.8 36.4 %copy-start = (bf16[1,192,768]{2,1,0:T(8,128)(2,1)S(1)}, bf16[1,192,768]{2,1,0:T(8,128)(2,1)}, u32[]{:S(2)}) copy-start(bf16[1,192,768]{2,1,0:T(8,128)(2,1)} %param.4) | copy-start | bytes 884740
  1.8 36.4 %copy-start.1 = (bf16[1,192,768]{2,1,0:T(8,128)(2,1)S(1)}, bf16[1,192,768]{2,1,0:T(8,128)(2,1)}, u32[]{:S(2)}) copy-start(bf16[1,192,768]{2,1,0:T(8,128)(2,1)} %param.5) | copy-start | bytes 884740
  24.4 14.3 %collective-permute-start = (bf16[1536,384]{1,0:T(8,128)(2,1)S(1)}, bf16[1536,384]{1,0:T(8,128)(2,1)S(1)}, u32[]{:S(2)}, u32[]{:S(2)}) collective-permute-start(bf16[1536,384]{1,0:T(8,128)(2,1)S(1)} %bitcast.14), channel_id=1, source_target_pairs={{0,64},{64,0},{1,65},{65,1},{2,66},{66,2},{3,67},{67,3},{4,68},{68... | collective-permute-start | bytes 3538952 | tf_op jit(solution)/shard_map/ppermute | solution.py:180
  26.3 10.7 %collective-permute-start.1 = (bf16[96,768]{1,0:T(8,128)(2,1)S(1)}, bf16[96,768]{1,0:T(8,128)(2,1)S(1)}, u32[]{:S(2)}, u32[]{:S(2)}) collective-permute-start(bf16[96,768]{1,0:T(8,128)(2,1)S(1)} %get-tuple-element.13), channel_id=1, source_target_pairs={{0,1},{1,2},{2,3},{3,4},{4,5},{5,6},{6,7},{7,8},{8,9},{9,10},{10,1... | collective-permute-start | bytes 442376 | tf_op jit(solution)/shard_map/ppermute | solution.py:178
  30.1 8.0 %collective-permute-start.2 = (bf16[96,768]{1,0:T(8,128)(2,1)S(1)}, bf16[96,768]{1,0:T(8,128)(2,1)S(1)}, u32[]{:S(2)}, u32[]{:S(2)}) collective-permute-start(bf16[96,768]{1,0:T(8,128)(2,1)S(1)} %get-tuple-element.14), channel_id=1, source_target_pairs={{1,0},{2,1},{3,2},{4,3},{5,4},{6,5},{7,6},{8,7},{9,8},{10,9},{11,1... | collective-permute-start | bytes 442376 | tf_op jit(solution)/shard_map/ppermute | solution.py:177
  38.7 1.0 copy-start.4
  43.3 0.7 copy-start.2
  43.9 4.7 %collective-permute-start.3 = (bf16[8,192,384]{2,1,0:T(8,128)(2,1)S(1)}, bf16[8,192,384]{2,1,0:T(8,128)(2,1)S(1)}, u32[]{:S(2)}, u32[]{:S(2)}) collective-permute-start(bf16[8,192,384]{2,1,0:T(8,128)(2,1)S(1)} %get-tuple-element.20), channel_id=1, source_target_pairs={{0,64},{64,0},{1,65},{65,1},{2,66},{66,2},{3,67},{67,3},{4,68},{68... | collective-permute-start | bytes 3538952 | tf_op jit(solution)/shard_map/ppermute | solution.py:211
  90.2 44.8 %copy-start.3 = (bf16[256,384]{1,0:T(8,128)(2,1)S(1)}, bf16[256,384]{1,0:T(8,128)(2,1)}, u32[]{:S(2)}) copy-start(bf16[256,384]{1,0:T(8,128)(2,1)} %copy-done.2) | copy-start | bytes 589828
  129.9 11.5 %all-to-all-start.3 = ((f32[4,48,384]{2,1,0:T(8,128)}), f32[4,48,384]{2,1,0:T(8,128)S(1)}, u32[]{:S(2)}, u32[]{:S(2)}) async-start(f32[4,48,384]{2,1,0:T(8,128)} %broadcast_in_dim.10), calls=%async_computation.3 | async-start | bytes 589824 | tf_op jit(solution)/shard_map/all_to_all | solution.py:137

commit v2 on v1

--- a/solution.py
+++ b/solution.py
@@ -67,7 +67,7 @@
     wide[SPAN + n :] = after[h:]
 
 
-def main_body(c_ref, near, far, act, wide, delta, wk, mine, send, wp_s, dk_s, dp_s):
+def main_body(c_ref, near, far, act, wide, delta, wk, mine, send, wp_s):
     c = c_ref[0]
     groups, _, ci = near.shape
     taps, channels, _ = wk.shape
@@ -90,22 +90,45 @@
     upstream = dot(wide[...], wp_s[...].astype(BF16), 1, 1)
     deltas = (upstream * slope).astype(BF16)
     delta[...] = deltas
-    dp_s[...] = dot(hidden[SPAN : SPAN + n].astype(BF16), wide[SPAN : SPAN + n], 0, 0)
     inner = deltas[SPAN : SPAN + n]
+
+    def place(v, at, pieces):
+        count = v.shape[0] // (2 * groups)
+        for core in range(2):
+
+            @pl.when(c == core)
+            def _():
+                for i in range(groups):
+                    own, other = (2 * i + core) * count, (2 * i + 1 - core) * count
+                    mine[i, at : at + pieces * count] = halves(v[own : own + count], pieces)
+                    send[i, at : at + pieces * count] = halves(v[other : other + count], pieces).astype(BF16)
+
+    place(dot(hidden[SPAN : SPAN + n].astype(BF16), wide[SPAN : SPAN + n], 0, 0), taps * rows, 2)
     for k in range(taps):
-        dk_s[k] = dot(act[(k + 1) * SPAN : (k + 1) * SPAN + n], inner, 0, 0)
-    for ref, core in ((mine, c), (send, 1 - c)):
-        for i in range(groups):
-            d = 2 * i + core
-            for k in range(taps):
-                v = dk_s[k, pl.ds(pl.multiple_of(d * rows, rows), rows)]
-                ref[i, k * rows : (k + 1) * rows] = v.astype(ref.dtype)
-            at = pl.ds(pl.multiple_of(d * prow, prow), prow)
-            v = jnp.concatenate([dp_s[at, :ci], dp_s[at, ci:]], axis=0)
-            ref[i, taps * rows :] = v.astype(ref.dtype)
-
-
-def input_body(delta, wk, x, cot, out):
+        place(dot(act[(k + 1) * SPAN : (k + 1) * SPAN + n], inner, 0, 0), k * rows, 1)
+
+
+def halves(v, pieces):
+    width = v.shape[1] // pieces
+    return jnp.concatenate([v[:, k * width : (k + 1) * width] for k in range(pieces)], axis=0)
+
+
+def spread_body(parts, copies):
+    total = jnp.sum(parts[...].astype(F32), axis=0)
+    for i in range(copies.shape[0]):
+        copies[i] = total
+
+
+def finish_body(s, conv, point):
+    taps, rows, ci = conv.shape
+    for k in range(taps):
+        conv[k] = s[k * rows : (k + 1) * rows]
+    q, prow = taps * rows, point.shape[0]
+    point[:, :ci] = s[q : q + prow]
+    point[:, ci:] = s[q + prow :]
+
+
+def input_body(delta, wk, _, x, cot, out):
     taps, n = wk.shape[0], x.shape[0]
     grad = dot(delta[(taps - 1) * SPAN : (taps - 1) * SPAN + n], wk[0], 1, 1)
     for k in range(1, taps):
@@ -129,12 +152,6 @@
 
 def limit(mib):
     return pltpu.CompilerParams(vmem_limit_bytes=mib << 20)
-
-
-def copies_to(x, axis):
-    n = lax.axis_size(axis)
-    y = jnp.broadcast_to(x[None], (n,) + x.shape).reshape((n * x.shape[0],) + x.shape[1:])
-    return lax.all_to_all(y, axis, 0, 0, tiled=True)
 
 
 def exchanged_sum(x, axis):
@@ -171,7 +188,7 @@
         out_specs=[whole(groups, total, CI), whole(h + SPAN, C), whole(h + SPAN, C)],
         out_shape=[sds((groups, total, CI), BF16), sds((h + SPAN, C), BF16), sds((h + SPAN, C), BF16)],
         name="pack",
-        compiler_params=limit(14),
+        compiler_params=limit(2),
     )(*map(in_hbm, (jnp.swapaxes(dilated_kernel_weight, 0, 1), point_weight, x, x, cot, cot)))
 
     after = lax.ppermute(down, SEQ, [(i + 1, i) for i in range(seq - 1)])
@@ -181,44 +198,54 @@
     near, far = near.reshape(groups, total, CI), far.reshape(groups, total, CI)
 
     spec = pl.BlockSpec(memory_space=pltpu.VMEM)
-    far = in_hbm(far)
     act, wide = pl.pallas_call(
         act_body,
         in_specs=[spec] * 4,
         out_specs=[spec] * 2,
         out_shape=[sds((n + 2 * h, C), BF16), sds((n + h, C), BF16)],
         name="act",
-        compiler_params=limit(14),
+        compiler_params=limit(2),
     )(x, cot, before, after)
-    delta, wk, mine, send = pl.pallas_call(
+    delta, wk, mine, send, spare = pl.pallas_call(
         main_body,
         in_specs=[pl.BlockSpec(memory_space=pltpu.SMEM)] + [spec] * 4,
-        out_specs=[spec] * 4,
+        out_specs=[spec] * 5,
         out_shape=[
             sds((n + h, CI), BF16),
             sds((taps, C, CI), BF16),
             sds((groups, total, CI), F32),
             sds((groups, total, CI), BF16),
-        ],
-        scratch_shapes=[
-            pltpu.VMEM((CI, C), F32),
-            pltpu.VMEM((taps, C, CI), F32),
-            pltpu.VMEM((CI, C), F32),
+            sds((CI, C), F32),
         ],
         name="main",
-        compiler_params=limit(14),
+        compiler_params=limit(2),
     )(core.reshape(1).astype(jnp.int32), near, far, act, wide)
     got = lax.ppermute(send, "c", PAIR)
-    grad_input = pl.pallas_call(input_body, in_specs=[spec] * 4, out_shape=sds((n, C), BF16), name="input_grad", compiler_params=limit(14))(delta, wk, x, cot)
+    grad_input = pl.pallas_call(input_body, in_specs=[spec] * 5, out_shape=sds((n, C), BF16), name="input_grad", compiler_params=limit(2))(delta, wk, spare, x, cot)
 
     s = (mine + got.astype(F32)).astype(BF16).reshape(groups * total, CI)
-    s = exchanged_sum(s, ("xl", "y", "xh"))
-    s = exchanged_sum(s, "zl")
-    s = jnp.sum(lax.all_gather(s.astype(BF16), "zh", axis=0).astype(F32), axis=0)
-    s = copies_to(s, ("xh", "zl"))
-    owned_conv = jnp.swapaxes(s[: taps * rows].reshape(taps, rows, CI), 0, 1)
-    q = taps * rows
-    owned_point = jnp.concatenate([s[q : q + prow], s[q + prow :]], axis=1)
+    s = exchanged_sum(s, ("xl", "y", "xh", "zl"))
+    parts = lax.all_gather(s.astype(BF16), "zh", axis=0)
+    final = lax.axis_size("xh") * lax.axis_size("zl")
+    own = s.shape[0]
+    s = pl.pallas_call(
+        spread_body,
+        in_specs=[spec],
+        out_specs=spec,
+        out_shape=sds((final, own, CI), F32),
+        name="spread",
+        compiler_params=limit(2),
+    )(parts)
+    s = lax.all_to_all(s.reshape(final * own, CI), ("xh", "zl"), 0, 0, tiled=True)
+    conv, owned_point = pl.pallas_call(
+        finish_body,
+        in_specs=[spec],
+        out_specs=[spec] * 2,
+        out_shape=[sds((taps, rows, CI), F32), sds((prow, C), F32)],
+        name="finish",
+        compiler_params=limit(2),
+    )(s)
+    owned_conv = jnp.swapaxes(conv, 0, 1)
     return (grad_input[None], owned_conv, owned_point)
 
 

time: 143 us -> 140 us (0.979)
  the two profiles are of different devices: /device:TPU:32 before, /device:TPU:2 now
where the time goes in v2:
time: 140 us
  blocking collectives  101 us (72%)
  waiting for transfers between devices  13.6 us (10%)
  starting transfers between devices  10.3 us (7%)
  Pallas kernels  7.71 us (6%)
  local copies, waits for them, and re-layouts  5.29 us (4%)
    all_gather x1, blocking collectives, per_device(): parts = lax.all_gather(s.astype(BF16), 'zh', axis=0)  39.5 us
    all_to_all x1, blocking collectives, exchanged_sum(): y = lax.all_to_all(x, axis, 0, 0, tiled=True)  34.8 us
    all_to_all x1, blocking collectives, per_device(): lax.all_to_all(copies.reshape(groups * total, CI), ('xl', 'y'), 0, 0, til...  26.5 us
    unnamed x16, local copies, waits for them, and re-layouts  5.29 us
    ppermute x1, waiting for transfers between devices, per_device(): after = lax.ppermute(down, SEQ, [(i + 1, i) for i in range(seq - 1)])  4.12 us
    all_to_all x1, waiting for transfers between devices, per_device(): lax.all_to_all(s.reshape(final * own, CI), ('xh', 'zl'), 0, 0, tiled=True)  3.93 us
    all_to_all x1, starting transfers between devices, per_device(): lax.all_to_all(s.reshape(final * own, CI), ('xh', 'zl'), 0, 0, tiled=True)  3.87 us
    ppermute x1, waiting for transfers between devices, per_device(): got = lax.ppermute(send, 'c', PAIR)  2.81 us
  transfers between devices with their start and end apart: 5, of which 4 were waited for; matrix products, arithmetic and copies ran while one was open for 0% of the time, Pallas kernels for 2%

profile of v2, /device:TPU:2, one launch (start us, length us, event | category | flops | bytes accessed | tf_op | source)
XLA Modules:
  0.0 139.6 jit_solution(7415967505455950397)
XLA Ops:
  0.6 1.1 pack.1
  1.8 26.5 %all_to_all.26.near = bf16[8,192,384]{2,1,0:T(8,128)(2,1)S(1)} all-to-all(bf16[8,192,384]{2,1,0:T(8,128)(2,1)S(1)} %get-tuple-element.15), channel_id=1, replica_groups=mesh['xl'=2,'y'=4,'c'=2,'xh'=2,'zh'=16,'zl'=2] {'xl','y'}, dimensions={0} | all-to-all | bytes 2359296 | tf_op jit(solution)/shard_map/all_to_all | solution.py:196
  28.4 1.9 %collective-permute-start = (bf16[1536,384]{1,0:T(8,128)(2,1)S(1)}, bf16[1536,384]{1,0:T(8,128)(2,1)S(1)}, u32[]{:S(2)}, u32[]{:S(2)}) collective-permute-start(bf16[1536,384]{1,0:T(8,128)(2,1)S(1)} %bitcast.11), channel_id=1, source_target_pairs={{0,64},{64,0},{1,65},{65,1},{2,66},{66,2},{3,67},{67,3},{4,68},{68... | collective-permute-start | bytes 3538952 | tf_op jit(solution)/shard_map/ppermute | solution.py:197
  30.3 1.3 collective-permute-start.1
  31.6 1.3 collective-permute-start.2
  32.9 2.7 %collective-permute-done.1.before = bf16[96,768]{1,0:T(8,128)(2,1)S(1)} collective-permute-done((bf16[96,768]{1,0:T(8,128)(2,1)S(1)}, bf16[96,768]{1,0:T(8,128)(2,1)S(1)}, u32[]{:S(2)}, u32[]{:S(2)}) %collective-permute-start.1) | collective-permute-done | bytes 147488 | tf_op jit(solution)/shard_map/ppermute | solution.py:195
  35.6 4.1 %collective-permute-done.2.after = bf16[96,768]{1,0:T(8,128)(2,1)S(1)} collective-permute-done((bf16[96,768]{1,0:T(8,128)(2,1)S(1)}, bf16[96,768]{1,0:T(8,128)(2,1)S(1)}, u32[]{:S(2)}, u32[]{:S(2)}) %collective-permute-start.2) | collective-permute-done | bytes 147488 | tf_op jit(solution)/shard_map/ppermute | solution.py:194
  39.7 0.5 act.1
  40.2 1.0 copy-done.2
  41.3 1.3 copy-done.3
  42.5 2.8 %main.1 = (bf16[256,384]{1,0:T(8,128)(2,1)S(1)}, bf16[3,768,384]{2,1,0:T(8,128)(2,1)S(1)}, f32[8,192,384]{2,1,0:T(8,128)S(1)}, bf16[8,192,384]{2,1,0:T(8,128)(2,1)S(1)}, f32[384,768]{1,0:T(8,128)S(1)}) custom-call(s32[1]{0:T(128)} %bitcast.c_ref, bf16[8,192,384]{2,1,0:T(8,128)(2,1)S(1)} %all_to_all.26.near, bf16[8,192,384]{2,1,0:T(8,128)(2,1)S(1)} %bitcast.21, ...), custom_call_target="tpu_custom_call" | custom-call | tf_op jit(solution)/shard_map/main/pallas_call | solution.py:209
  45.4 1.0 copy-done.4
  46.4 0.7 copy-done.6
  47.1 1.9 %collective-permute-start.3 = (bf16[8,192,384]{2,1,0:T(8,128)(2,1)S(1)}, bf16[8,192,384]{2,1,0:T(8,128)(2,1)S(1)}, u32[]{:S(2)}, u32[]{:S(2)}) collective-permute-start(bf16[8,192,384]{2,1,0:T(8,128)(2,1)S(1)} %get-tuple-element.24), channel_id=1, source_target_pairs={{0,64},{64,0},{1,65},{65,1},{2,66},{66,2},{3,67},{67,3},{4,68},{68... | collective-permute-start | bytes 3538952 | tf_op jit(solution)/shard_map/ppermute | solution.py:223
  49.0 2.8 %collective-permute-done.3 = bf16[8,192,384]{2,1,0:T(8,128)(2,1)S(1)} collective-permute-done((bf16[8,192,384]{2,1,0:T(8,128)(2,1)S(1)}, bf16[8,192,384]{2,1,0:T(8,128)(2,1)S(1)}, u32[]{:S(2)}, u32[]{:S(2)}) %collective-permute-start.3) | collective-permute-done | bytes 1179680 | tf_op jit(solution)/shard_map/ppermute | solution.py:223
  52.1 34.8 %all_to_all.27 = bf16[32,48,384]{2,1,0:T(8,128)(2,1)S(1)} all-to-all(bf16[32,48,384]{2,1,0:T(8,128)(2,1)S(1)} %bitcast.23), channel_id=1, replica_groups=mesh['xl'=2,'y'=4,'c'=2,'xh'=2,'zh'=16,'zl'=2] {'xl','y','xh','zl'}, dimensions={0} | all-to-all | bytes 2359296 | tf_op jit(solution)/shard_map/all_to_all | solution.py:159
  86.9 0.8 reduce_sum.12
  87.7 39.5 %all-gather = bf16[768,384]{1,0:T(8,128)(2,1)S(1)} all-gather(bf16[48,384]{1,0:T(8,128)(2,1)} %reduce_sum.12), channel_id=2, replica_groups=mesh['xl'=2,'y'=4,'c'=2,'xh'=2,'zh'=16,'zl'=2] {'zh'}, dimensions={0}, use_global_device_ids=true | all-gather | bytes 626688 | tf_op jit(solution)/shard_map/all_gather | solution.py:228
  127.2 0.8 spread.1
  128.0 3.9 %all-to-all-start.2 = ((f32[4,48,384]{2,1,0:T(8,128)}), f32[4,48,384]{2,1,0:T(8,128)S(1)}, u32[]{:S(2)}, u32[]{:S(2)}) async-start(f32[4,48,384]{2,1,0:T(8,128)} %spread.1), calls=%async_computation.2 | async-start | bytes 589824 | tf_op jit(solution)/shard_map/all_to_all | solution.py:239
  131.9 1.3 copy-done.5
  133.2 1.8 %input_grad.1 = bf16[192,768]{1,0:T(8,128)(2,1)} custom-call(bf16[256,384]{1,0:T(8,128)(2,1)S(1)} %copy-done.7, bf16[3,768,384]{2,1,0:T(8,128)(2,1)S(1)} %get-tuple-element.21.wk, f32[384,768]{1,0:T(8,128)S(1)} %copy-done.5, bf16[192,768]{1,0:T(8,128)(2,1)S(1)} %bitcast.15, bf16[192,768]{1,0:T(8,128)(2,1)S(1)} %bitcast.19), custom_call_target="tpu_custom_call" | custom-call | tf_op jit(solution)/shard_map/input_grad/pallas_call | solution.py:224
  134.9 3.9 %all-to-all-done.2 = f32[4,48,384]{2,1,0:T(8,128)S(1)} async-done(((f32[4,48,384]{2,1,0:T(8,128)}), f32[4,48,384]{2,1,0:T(8,128)S(1)}, u32[]{:S(2)}, u32[]{:S(2)}) %all-to-all-start.2) | async-done | bytes 294944 | tf_op jit(solution)/shard_map/all_to_all | solution.py:239
  138.9 0.7 finish.1
  (13 shorter events, 0.4 us)
Async XLA Ops:
  1.8 37.9 %copy-start = (bf16[1,192,768]{2,1,0:T(8,128)(2,1)S(1)}, bf16[1,192,768]{2,1,0:T(8,128)(2,1)}, u32[]{:S(2)}) copy-start(bf16[1,192,768]{2,1,0:T(8,128)(2,1)} %param.4) | copy-start | bytes 884740
  1.8 37.9 %copy-start.1 = (bf16[1,192,768]{2,1,0:T(8,128)(2,1)S(1)}, bf16[1,192,768]{2,1,0:T(8,128)(2,1)}, u32[]{:S(2)}) copy-start(bf16[1,192,768]{2,1,0:T(8,128)(2,1)} %param.5) | copy-start | bytes 884740
  28.4 11.8 %collective-permute-start = (bf16[1536,384]{1,0:T(8,128)(2,1)S(1)}, bf16[1536,384]{1,0:T(8,128)(2,1)S(1)}, u32[]{:S(2)}, u32[]{:S(2)}) collective-permute-start(bf16[1536,384]{1,0:T(8,128)(2,1)S(1)} %bitcast.11), channel_id=1, source_target_pairs={{0,64},{64,0},{1,65},{65,1},{2,66},{66,2},{3,67},{67,3},{4,68},{68... | collective-permute-start | bytes 3538952 | tf_op jit(solution)/shard_map/ppermute | solution.py:197
  30.3 5.3 %collective-permute-start.1 = (bf16[96,768]{1,0:T(8,128)(2,1)S(1)}, bf16[96,768]{1,0:T(8,128)(2,1)S(1)}, u32[]{:S(2)}, u32[]{:S(2)}) collective-permute-start(bf16[96,768]{1,0:T(8,128)(2,1)S(1)} %get-tuple-element.16), channel_id=1, source_target_pairs={{0,1},{1,2},{2,3},{3,4},{4,5},{5,6},{6,7},{7,8},{8,9},{9,10},{10,1... | collective-permute-start | bytes 442376 | tf_op jit(solution)/shard_map/ppermute | solution.py:195
  31.6 8.1 %collective-permute-start.2 = (bf16[96,768]{1,0:T(8,128)(2,1)S(1)}, bf16[96,768]{1,0:T(8,128)(2,1)S(1)}, u32[]{:S(2)}, u32[]{:S(2)}) collective-permute-start(bf16[96,768]{1,0:T(8,128)(2,1)S(1)} %get-tuple-element.17), channel_id=1, source_target_pairs={{1,0},{2,1},{3,2},{4,3},{5,4},{6,5},{7,6},{8,7},{9,8},{10,9},{11,1... | collective-permute-start | bytes 442376 | tf_op jit(solution)/shard_map/ppermute | solution.py:194
  40.2 1.0 copy-start.2
  41.3 1.3 copy-start.3
  45.3 1.0 copy-start.4
  46.4 0.7 copy-start.6
  47.1 4.7 %collective-permute-start.3 = (bf16[8,192,384]{2,1,0:T(8,128)(2,1)S(1)}, bf16[8,192,384]{2,1,0:T(8,128)(2,1)S(1)}, u32[]{:S(2)}, u32[]{:S(2)}) collective-permute-start(bf16[8,192,384]{2,1,0:T(8,128)(2,1)S(1)} %get-tuple-element.24), channel_id=1, source_target_pairs={{0,64},{64,0},{1,65},{65,1},{2,66},{66,2},{3,67},{67,3},{4,68},{68... | collective-permute-start | bytes 3538952 | tf_op jit(solution)/shard_map/ppermute | solution.py:223
  87.7 44.2 %copy-start.7 = (bf16[256,384]{1,0:T(8,128)(2,1)S(1)}, bf16[256,384]{1,0:T(8,128)(2,1)}, u32[]{:S(2)}) copy-start(bf16[256,384]{1,0:T(8,128)(2,1)} %copy-done.6) | copy-start | bytes 589828
  128.0 10.8 %all-to-all-start.2 = ((f32[4,48,384]{2,1,0:T(8,128)}), f32[4,48,384]{2,1,0:T(8,128)S(1)}, u32[]{:S(2)}, u32[]{:S(2)}) async-start(f32[4,48,384]{2,1,0:T(8,128)} %spread.1), calls=%async_computation.2 | async-start | bytes 589824 | tf_op jit(solution)/shard_map/all_to_all | solution.py:239
  131.9 1.3 copy-start.5

commit v3 on v2

--- a/solution.py
+++ b/solution.py
@@ -52,7 +52,11 @@
     down[2 * SPAN :] = ca[...]
 
 
-def act_body(x, cot, before, after, act, wide):
+def settle_body(before, after, mark):
+    mark[...] = before[...].astype(F32) + after[...].astype(F32)
+
+
+def act_body(_, x, cot, before, after, act, wide):
     n, h = x.shape[0], 2 * SPAN
 
     def part(v):
@@ -198,14 +202,24 @@
     near, far = near.reshape(groups, total, CI), far.reshape(groups, total, CI)
 
     spec = pl.BlockSpec(memory_space=pltpu.VMEM)
+    tile = pl.BlockSpec((16, 128), lambda i: (0, 0))
+    mark = pl.pallas_call(
+        settle_body,
+        grid=(1,),
+        in_specs=[tile] * 2,
+        out_specs=tile,
+        out_shape=sds((16, 128), F32),
+        name="settle",
+        compiler_params=limit(2),
+    )(before, after)
     act, wide = pl.pallas_call(
         act_body,
-        in_specs=[spec] * 4,
+        in_specs=[spec] * 5,
         out_specs=[spec] * 2,
         out_shape=[sds((n + 2 * h, C), BF16), sds((n + h, C), BF16)],
         name="act",
         compiler_params=limit(2),
-    )(x, cot, before, after)
+    )(mark, x, cot, before, after)
     delta, wk, mine, send, spare = pl.pallas_call(
         main_body,
         in_specs=[pl.BlockSpec(memory_space=pltpu.SMEM)] + [spec] * 4,

time: 140 us -> 140 us (level)
  the two profiles are of different devices: /device:TPU:2 before, /device:TPU:8 now
where the time goes in v3:
time: 140 us
  blocking collectives  101 us (72%)
  waiting for transfers between devices  13.6 us (10%)
  starting transfers between devices  10.6 us (8%)
  Pallas kernels  7.72 us (6%)
  local copies, waits for them, and re-layouts  5.29 us (4%)
    all_gather x1, blocking collectives, per_device(): parts = lax.all_gather(s.astype(BF16), 'zh', axis=0)  39.7 us
    all_to_all x1, blocking collectives, exchanged_sum(): y = lax.all_to_all(x, axis, 0, 0, tiled=True)  34.9 us
    all_to_all x1, blocking collectives, per_device(): lax.all_to_all(copies.reshape(groups * total, CI), ('xl', 'y'), 0, 0, til...  26.3 us
    unnamed x16, local copies, waits for them, and re-layouts  5.29 us
    all_to_all x1, starting transfers between devices, per_device(): lax.all_to_all(s.reshape(final * own, CI), ('xh', 'zl'), 0, 0, tiled=True)  4.23 us
    ppermute x1, waiting for transfers between devices, per_device(): after = lax.ppermute(down, SEQ, [(i + 1, i) for i in range(seq - 1)])  4.12 us
    all_to_all x1, waiting for transfers between devices, per_device(): lax.all_to_all(s.reshape(final * own, CI), ('xh', 'zl'), 0, 0, tiled=True)  3.92 us
    ppermute x1, waiting for transfers between devices, per_device(): got = lax.ppermute(send, 'c', PAIR)  2.81 us
  transfers between devices with their start and end apart: 5, of which 4 were waited for; matrix products, arithmetic and copies ran while one was open for 0% of the time, Pallas kernels for 2%

profile of v3, /device:TPU:8, one launch (start us, length us, event | category | flops | bytes accessed | tf_op | source)
XLA Modules:
  0.0 140.0 jit_solution(656186797604813156)
XLA Ops:
  0.6 1.1 pack.1
  1.8 26.3 %all_to_all.26.near = bf16[8,192,384]{2,1,0:T(8,128)(2,1)S(1)} all-to-all(bf16[8,192,384]{2,1,0:T(8,128)(2,1)S(1)} %get-tuple-element.15), channel_id=1, replica_groups=mesh['xl'=2,'y'=4,'c'=2,'xh'=2,'zh'=16,'zl'=2] {'xl','y'}, dimensions={0} | all-to-all | bytes 2359296 | tf_op jit(solution)/shard_map/all_to_all | solution.py:200
  28.1 1.9 %collective-permute-start = (bf16[1536,384]{1,0:T(8,128)(2,1)S(1)}, bf16[1536,384]{1,0:T(8,128)(2,1)S(1)}, u32[]{:S(2)}, u32[]{:S(2)}) collective-permute-start(bf16[1536,384]{1,0:T(8,128)(2,1)S(1)} %bitcast.11), channel_id=1, source_target_pairs={{0,64},{64,0},{1,65},{65,1},{2,66},{66,2},{3,67},{67,3},{4,68},{68... | collective-permute-start | bytes 3538952 | tf_op jit(solution)/shard_map/ppermute | solution.py:201
  30.0 1.3 collective-permute-start.1
  31.3 1.3 collective-permute-start.2
  32.6 2.7 %collective-permute-done.1.before = bf16[96,768]{1,0:T(8,128)(2,1)S(1)} collective-permute-done((bf16[96,768]{1,0:T(8,128)(2,1)S(1)}, bf16[96,768]{1,0:T(8,128)(2,1)S(1)}, u32[]{:S(2)}, u32[]{:S(2)}) %collective-permute-start.1) | collective-permute-done | bytes 147488 | tf_op jit(solution)/shard_map/ppermute | solution.py:199
  35.4 4.1 %collective-permute-done.2.after = bf16[96,768]{1,0:T(8,128)(2,1)S(1)} collective-permute-done((bf16[96,768]{1,0:T(8,128)(2,1)S(1)}, bf16[96,768]{1,0:T(8,128)(2,1)S(1)}, u32[]{:S(2)}, u32[]{:S(2)}) %collective-permute-start.2) | collective-permute-done | bytes 147488 | tf_op jit(solution)/shard_map/ppermute | solution.py:198
  39.5 0.5 act.1
  40.0 1.0 copy-done.2
  41.0 1.3 copy-done.3
  42.3 2.8 %main.1 = (bf16[256,384]{1,0:T(8,128)(2,1)S(1)}, bf16[3,768,384]{2,1,0:T(8,128)(2,1)S(1)}, f32[8,192,384]{2,1,0:T(8,128)S(1)}, bf16[8,192,384]{2,1,0:T(8,128)(2,1)S(1)}, f32[384,768]{1,0:T(8,128)S(1)}) custom-call(s32[1]{0:T(128)} %bitcast.c_ref, bf16[8,192,384]{2,1,0:T(8,128)(2,1)S(1)} %all_to_all.26.near, bf16[8,192,384]{2,1,0:T(8,128)(2,1)S(1)} %bitcast.21, ...), custom_call_target="tpu_custom_call" | custom-call | tf_op jit(solution)/shard_map/main/pallas_call | solution.py:223
  45.1 1.0 copy-done.4
  46.1 0.7 copy-done.6
  46.8 1.9 %collective-permute-start.3 = (bf16[8,192,384]{2,1,0:T(8,128)(2,1)S(1)}, bf16[8,192,384]{2,1,0:T(8,128)(2,1)S(1)}, u32[]{:S(2)}, u32[]{:S(2)}) collective-permute-start(bf16[8,192,384]{2,1,0:T(8,128)(2,1)S(1)} %get-tuple-element.24), channel_id=1, source_target_pairs={{0,64},{64,0},{1,65},{65,1},{2,66},{66,2},{3,67},{67,3},{4,68},{68... | collective-permute-start | bytes 3538952 | tf_op jit(solution)/shard_map/ppermute | solution.py:237
  48.7 2.8 %collective-permute-done.3 = bf16[8,192,384]{2,1,0:T(8,128)(2,1)S(1)} collective-permute-done((bf16[8,192,384]{2,1,0:T(8,128)(2,1)S(1)}, bf16[8,192,384]{2,1,0:T(8,128)(2,1)S(1)}, u32[]{:S(2)}, u32[]{:S(2)}) %collective-permute-start.3) | collective-permute-done | bytes 1179680 | tf_op jit(solution)/shard_map/ppermute | solution.py:237
  51.9 34.9 %all_to_all.27 = bf16[32,48,384]{2,1,0:T(8,128)(2,1)S(1)} all-to-all(bf16[32,48,384]{2,1,0:T(8,128)(2,1)S(1)} %bitcast.23), channel_id=1, replica_groups=mesh['xl'=2,'y'=4,'c'=2,'xh'=2,'zh'=16,'zl'=2] {'xl','y','xh','zl'}, dimensions={0} | all-to-all | bytes 2359296 | tf_op jit(solution)/shard_map/all_to_all | solution.py:163
  86.8 0.8 reduce_sum.12
  87.5 39.7 %all-gather = bf16[768,384]{1,0:T(8,128)(2,1)S(1)} all-gather(bf16[48,384]{1,0:T(8,128)(2,1)} %reduce_sum.12), channel_id=2, replica_groups=mesh['xl'=2,'y'=4,'c'=2,'xh'=2,'zh'=16,'zl'=2] {'zh'}, dimensions={0}, use_global_device_ids=true | all-gather | bytes 626688 | tf_op jit(solution)/shard_map/all_gather | solution.py:242
  127.3 0.8 spread.1
  128.1 4.2 %all-to-all-start.2 = ((f32[4,48,384]{2,1,0:T(8,128)}), f32[4,48,384]{2,1,0:T(8,128)S(1)}, u32[]{:S(2)}, u32[]{:S(2)}) async-start(f32[4,48,384]{2,1,0:T(8,128)} %spread.1), calls=%async_computation.2 | async-start | bytes 589824 | tf_op jit(solution)/shard_map/all_to_all | solution.py:253
  132.3 1.3 copy-done.5
  133.6 1.8 %input_grad.1 = bf16[192,768]{1,0:T(8,128)(2,1)} custom-call(bf16[256,384]{1,0:T(8,128)(2,1)S(1)} %copy-done.7, bf16[3,768,384]{2,1,0:T(8,128)(2,1)S(1)} %get-tuple-element.21.wk, f32[384,768]{1,0:T(8,128)S(1)} %copy-done.5, bf16[192,768]{1,0:T(8,128)(2,1)S(1)} %bitcast.15, bf16[192,768]{1,0:T(8,128)(2,1)S(1)} %bitcast.19), custom_call_target="tpu_custom_call" | custom-call | tf_op jit(solution)/shard_map/input_grad/pallas_call | solution.py:238
  135.3 3.9 %all-to-all-done.2 = f32[4,48,384]{2,1,0:T(8,128)S(1)} async-done(((f32[4,48,384]{2,1,0:T(8,128)}), f32[4,48,384]{2,1,0:T(8,128)S(1)}, u32[]{:S(2)}, u32[]{:S(2)}) %all-to-all-start.2) | async-done | bytes 294944 | tf_op jit(solution)/shard_map/all_to_all | solution.py:253
  139.3 0.7 finish.1
  (14 shorter events, 0.4 us)
Async XLA Ops:
  1.8 37.7 %copy-start = (bf16[1,192,768]{2,1,0:T(8,128)(2,1)S(1)}, bf16[1,192,768]{2,1,0:T(8,128)(2,1)}, u32[]{:S(2)}) copy-start(bf16[1,192,768]{2,1,0:T(8,128)(2,1)} %param.4) | copy-start | bytes 884740
  1.8 37.7 %copy-start.1 = (bf16[1,192,768]{2,1,0:T(8,128)(2,1)S(1)}, bf16[1,192,768]{2,1,0:T(8,128)(2,1)}, u32[]{:S(2)}) copy-start(bf16[1,192,768]{2,1,0:T(8,128)(2,1)} %param.5) | copy-start | bytes 884740
  28.1 11.9 %collective-permute-start = (bf16[1536,384]{1,0:T(8,128)(2,1)S(1)}, bf16[1536,384]{1,0:T(8,128)(2,1)S(1)}, u32[]{:S(2)}, u32[]{:S(2)}) collective-permute-start(bf16[1536,384]{1,0:T(8,128)(2,1)S(1)} %bitcast.11), channel_id=1, source_target_pairs={{0,64},{64,0},{1,65},{65,1},{2,66},{66,2},{3,67},{67,3},{4,68},{68... | collective-permute-start | bytes 3538952 | tf_op jit(solution)/shard_map/ppermute | solution.py:201
  30.0 5.3 %collective-permute-start.1 = (bf16[96,768]{1,0:T(8,128)(2,1)S(1)}, bf16[96,768]{1,0:T(8,128)(2,1)S(1)}, u32[]{:S(2)}, u32[]{:S(2)}) collective-permute-start(bf16[96,768]{1,0:T(8,128)(2,1)S(1)} %get-tuple-element.16), channel_id=1, source_target_pairs={{0,1},{1,2},{2,3},{3,4},{4,5},{5,6},{6,7},{7,8},{8,9},{9,10},{10,1... | collective-permute-start | bytes 442376 | tf_op jit(solution)/shard_map/ppermute | solution.py:199
  31.3 8.1 %collective-permute-start.2 = (bf16[96,768]{1,0:T(8,128)(2,1)S(1)}, bf16[96,768]{1,0:T(8,128)(2,1)S(1)}, u32[]{:S(2)}, u32[]{:S(2)}) collective-permute-start(bf16[96,768]{1,0:T(8,128)(2,1)S(1)} %get-tuple-element.17), channel_id=1, source_target_pairs={{1,0},{2,1},{3,2},{4,3},{5,4},{6,5},{7,6},{8,7},{9,8},{10,9},{11,1... | collective-permute-start | bytes 442376 | tf_op jit(solution)/shard_map/ppermute | solution.py:198
  40.0 1.0 copy-start.2
  41.0 1.3 copy-start.3
  45.1 1.0 copy-start.4
  46.1 0.7 copy-start.6
  46.8 4.7 %collective-permute-start.3 = (bf16[8,192,384]{2,1,0:T(8,128)(2,1)S(1)}, bf16[8,192,384]{2,1,0:T(8,128)(2,1)S(1)}, u32[]{:S(2)}, u32[]{:S(2)}) collective-permute-start(bf16[8,192,384]{2,1,0:T(8,128)(2,1)S(1)} %get-tuple-element.24), channel_id=1, source_target_pairs={{0,64},{64,0},{1,65},{65,1},{2,66},{66,2},{3,67},{67,3},{4,68},{68... | collective-permute-start | bytes 3538952 | tf_op jit(solution)/shard_map/ppermute | solution.py:237
  87.5 44.7 %copy-start.7 = (bf16[256,384]{1,0:T(8,128)(2,1)S(1)}, bf16[256,384]{1,0:T(8,128)(2,1)}, u32[]{:S(2)}) copy-start(bf16[256,384]{1,0:T(8,128)(2,1)} %copy-done.6) | copy-start | bytes 589828
  128.1 11.2 %all-to-all-start.2 = ((f32[4,48,384]{2,1,0:T(8,128)}), f32[4,48,384]{2,1,0:T(8,128)S(1)}, u32[]{:S(2)}, u32[]{:S(2)}) async-start(f32[4,48,384]{2,1,0:T(8,128)} %spread.1), calls=%async_computation.2 | async-start | bytes 589824 | tf_op jit(solution)/shard_map/all_to_all | solution.py:253
  132.3 1.3 copy-start.5

commit v4 on v3

--- a/solution.py
+++ b/solution.py
@@ -37,19 +37,20 @@
     return lax.rsqrt(jnp.mean(x * x, axis=-1, keepdims=True) + EPS)
 
 
-def pack_body(wk, wp, xa, xb, ca, cb, copies, up, down):
-    taps, rows, ci = wk.shape
-    w = [wk[k] for k in range(taps)]
-    p = wp[...].astype(F32)
-    p = jnp.concatenate([p[:, :ci], p[:, ci:]], axis=0).astype(BF16)
-    for i in range(copies.shape[0]):
-        for k in range(taps):
-            copies[i, k * rows : (k + 1) * rows] = w[k]
-        copies[i, taps * rows :] = p
+def pack_body(wk, wp, xa, xb, ca, cb, copies, up, down, tile, sems):
+    taps, rows, _ = wk.shape
+    for k in range(taps):
+        tile[k * rows : (k + 1) * rows] = wk[k]
+    tile[taps * rows :] = halves(wp[...].astype(F32), 2).astype(BF16)
+    sends = [pltpu.make_async_copy(tile, copies.at[i], sems.at[i]) for i in range(copies.shape[0])]
+    for send in sends:
+        send.start()
     up[: 2 * SPAN] = xb[...]
     up[2 * SPAN :] = cb[...]
     down[: 2 * SPAN] = xa[...]
     down[2 * SPAN :] = ca[...]
+    for send in sends:
+        send.wait()
 
 
 def settle_body(before, after, mark):
@@ -189,8 +190,9 @@
             pl.BlockSpec((SPAN, C), lambda i: (0, 0)),
             pl.BlockSpec((SPAN, C), lambda i: (edge, 0)),
         ],
-        out_specs=[whole(groups, total, CI), whole(h + SPAN, C), whole(h + SPAN, C)],
+        out_specs=[pl.BlockSpec(memory_space=pltpu.HBM), whole(h + SPAN, C), whole(h + SPAN, C)],
         out_shape=[sds((groups, total, CI), BF16), sds((h + SPAN, C), BF16), sds((h + SPAN, C), BF16)],
+        scratch_shapes=[pltpu.VMEM((total, CI), BF16), pltpu.SemaphoreType.DMA((groups,))],
         name="pack",
         compiler_params=limit(2),
     )(*map(in_hbm, (jnp.swapaxes(dilated_kernel_weight, 0, 1), point_weight, x, x, cot, cot)))

time: 140 us -> 142 us (1.014)
  the two profiles are of different devices: /device:TPU:8 before, /device:TPU:2 now
where the time goes in v4:
time: 142 us; the launch traced here: 141 us
  blocking collectives  101 us (71%)
  waiting for transfers between devices  13.6 us (10%)
  starting transfers between devices  10.4 us (7%)
  Pallas kernels  9.24 us (7%)
  local copies, waits for them, and re-layouts  5.29 us (4%)
    all_gather x1, blocking collectives, per_device(): parts = lax.all_gather(s.astype(BF16), 'zh', axis=0)  39.5 us
    all_to_all x1, blocking collectives, exchanged_sum(): y = lax.all_to_all(x, axis, 0, 0, tiled=True)  34.8 us
    all_to_all x1, blocking collectives, per_device(): lax.all_to_all(copies.reshape(groups * total, CI), ('xl', 'y'), 0, 0, til...  26.5 us
    unnamed x16, local copies, waits for them, and re-layouts  5.29 us
    ppermute x1, waiting for transfers between devices, per_device(): after = lax.ppermute(down, SEQ, [(i + 1, i) for i in range(seq - 1)])  4.12 us
    all_to_all x1, starting transfers between devices, per_device(): lax.all_to_all(s.reshape(final * own, CI), ('xh', 'zl'), 0, 0, tiled=True)  4 us
    all_to_all x1, waiting for transfers between devices, per_device(): lax.all_to_all(s.reshape(final * own, CI), ('xh', 'zl'), 0, 0, tiled=True)  3.92 us
  transfers between devices with their start and end apart: 5, of which 4 were waited for; matrix products, arithmetic and copies ran while one was open for 0% of the time, Pallas kernels for 2%

profile of v4, /device:TPU:2, one launch (start us, length us, event | category | flops | bytes accessed | tf_op | source)
XLA Modules:
  0.0 141.2 jit_solution(4463364681501773790)
XLA Ops:
  0.6 2.7 %pack.1 = (bf16[8,192,384]{2,1,0:T(8,128)(2,1)S(1)}, bf16[96,768]{1,0:T(8,128)(2,1)S(1)}, bf16[96,768]{1,0:T(8,128)(2,1)S(1)}) custom-call(bf16[3,48,384]{2,1,0:T(8,128)(2,1)} %bitcast.25, bf16[24,768]{1,0:T(8,128)(2,1)} %wp.1, bf16[192,768]{1,0:T(8,128)(2,1)} %bitcast.12, bf16[192,768]{1,0:T(8,128)(2,1)} %bitcast.13, bf16[192,768]{1,0:T(8,128)(2,1)} %bitcast.16, ...), custom_call_target="tpu_custom_call" | custom-call | tf_op jit(solution)/shard_map/pack/pallas_call | solution.py:182
  3.3 26.5 %all_to_all.26.near = bf16[8,192,384]{2,1,0:T(8,128)(2,1)S(1)} all-to-all(bf16[8,192,384]{2,1,0:T(8,128)(2,1)S(1)} %get-tuple-element.15), channel_id=1, replica_groups=mesh['xl'=2,'y'=4,'c'=2,'xh'=2,'zh'=16,'zl'=2] {'xl','y'}, dimensions={0} | all-to-all | bytes 2359296 | tf_op jit(solution)/shard_map/all_to_all | solution.py:202
  29.9 1.9 %collective-permute-start = (bf16[1536,384]{1,0:T(8,128)(2,1)S(1)}, bf16[1536,384]{1,0:T(8,128)(2,1)S(1)}, u32[]{:S(2)}, u32[]{:S(2)}) collective-permute-start(bf16[1536,384]{1,0:T(8,128)(2,1)S(1)} %bitcast.11), channel_id=1, source_target_pairs={{0,64},{64,0},{1,65},{65,1},{2,66},{66,2},{3,67},{67,3},{4,68},{68... | collective-permute-start | bytes 3538952 | tf_op jit(solution)/shard_map/ppermute | solution.py:203
  31.8 1.3 collective-permute-start.1
  33.1 1.3 collective-permute-start.2
  34.4 2.7 %collective-permute-done.1.before = bf16[96,768]{1,0:T(8,128)(2,1)S(1)} collective-permute-done((bf16[96,768]{1,0:T(8,128)(2,1)S(1)}, bf16[96,768]{1,0:T(8,128)(2,1)S(1)}, u32[]{:S(2)}, u32[]{:S(2)}) %collective-permute-start.1) | collective-permute-done | bytes 147488 | tf_op jit(solution)/shard_map/ppermute | solution.py:201
  37.1 4.1 %collective-permute-done.2.after = bf16[96,768]{1,0:T(8,128)(2,1)S(1)} collective-permute-done((bf16[96,768]{1,0:T(8,128)(2,1)S(1)}, bf16[96,768]{1,0:T(8,128)(2,1)S(1)}, u32[]{:S(2)}, u32[]{:S(2)}) %collective-permute-start.2) | collective-permute-done | bytes 147488 | tf_op jit(solution)/shard_map/ppermute | solution.py:200
  41.3 0.5 act.1
  41.8 1.0 copy-done.2
  42.8 1.3 copy-done.3
  44.1 2.8 %main.1 = (bf16[256,384]{1,0:T(8,128)(2,1)S(1)}, bf16[3,768,384]{2,1,0:T(8,128)(2,1)S(1)}, f32[8,192,384]{2,1,0:T(8,128)S(1)}, bf16[8,192,384]{2,1,0:T(8,128)(2,1)S(1)}, f32[384,768]{1,0:T(8,128)S(1)}) custom-call(s32[1]{0:T(128)} %bitcast.c_ref, bf16[8,192,384]{2,1,0:T(8,128)(2,1)S(1)} %all_to_all.26.near, bf16[8,192,384]{2,1,0:T(8,128)(2,1)S(1)} %bitcast.21, ...), custom_call_target="tpu_custom_call" | custom-call | tf_op jit(solution)/shard_map/main/pallas_call | solution.py:225
  46.9 1.0 copy-done.4
  47.9 0.7 copy-done.6
  48.6 1.9 %collective-permute-start.3 = (bf16[8,192,384]{2,1,0:T(8,128)(2,1)S(1)}, bf16[8,192,384]{2,1,0:T(8,128)(2,1)S(1)}, u32[]{:S(2)}, u32[]{:S(2)}) collective-permute-start(bf16[8,192,384]{2,1,0:T(8,128)(2,1)S(1)} %get-tuple-element.24), channel_id=1, source_target_pairs={{0,64},{64,0},{1,65},{65,1},{2,66},{66,2},{3,67},{67,3},{4,68},{68... | collective-permute-start | bytes 3538952 | tf_op jit(solution)/shard_map/ppermute | solution.py:239
  50.5 2.8 %collective-permute-done.3 = bf16[8,192,384]{2,1,0:T(8,128)(2,1)S(1)} collective-permute-done((bf16[8,192,384]{2,1,0:T(8,128)(2,1)S(1)}, bf16[8,192,384]{2,1,0:T(8,128)(2,1)S(1)}, u32[]{:S(2)}, u32[]{:S(2)}) %collective-permute-start.3) | collective-permute-done | bytes 1179680 | tf_op jit(solution)/shard_map/ppermute | solution.py:239
  53.7 34.8 %all_to_all.27 = bf16[32,48,384]{2,1,0:T(8,128)(2,1)S(1)} all-to-all(bf16[32,48,384]{2,1,0:T(8,128)(2,1)S(1)} %bitcast.23), channel_id=1, replica_groups=mesh['xl'=2,'y'=4,'c'=2,'xh'=2,'zh'=16,'zl'=2] {'xl','y','xh','zl'}, dimensions={0} | all-to-all | bytes 2359296 | tf_op jit(solution)/shard_map/all_to_all | solution.py:164
  88.4 0.8 reduce_sum.12
  89.2 39.5 %all-gather = bf16[768,384]{1,0:T(8,128)(2,1)S(1)} all-gather(bf16[48,384]{1,0:T(8,128)(2,1)} %reduce_sum.12), channel_id=2, replica_groups=mesh['xl'=2,'y'=4,'c'=2,'xh'=2,'zh'=16,'zl'=2] {'zh'}, dimensions={0}, use_global_device_ids=true | all-gather | bytes 626688 | tf_op jit(solution)/shard_map/all_gather | solution.py:244
  128.8 0.8 spread.1
  129.6 4.0 %all-to-all-start.2 = ((f32[4,48,384]{2,1,0:T(8,128)}), f32[4,48,384]{2,1,0:T(8,128)S(1)}, u32[]{:S(2)}, u32[]{:S(2)}) async-start(f32[4,48,384]{2,1,0:T(8,128)} %spread.1), calls=%async_computation.2 | async-start | bytes 589824 | tf_op jit(solution)/shard_map/all_to_all | solution.py:255
  133.6 1.3 copy-done.5
  134.8 1.8 %input_grad.1 = bf16[192,768]{1,0:T(8,128)(2,1)} custom-call(bf16[256,384]{1,0:T(8,128)(2,1)S(1)} %copy-done.7, bf16[3,768,384]{2,1,0:T(8,128)(2,1)S(1)} %get-tuple-element.21.wk, f32[384,768]{1,0:T(8,128)S(1)} %copy-done.5, bf16[192,768]{1,0:T(8,128)(2,1)S(1)} %bitcast.15, bf16[192,768]{1,0:T(8,128)(2,1)S(1)} %bitcast.19), custom_call_target="tpu_custom_call" | custom-call | tf_op jit(solution)/shard_map/input_grad/pallas_call | solution.py:240
  136.6 3.9 %all-to-all-done.2 = f32[4,48,384]{2,1,0:T(8,128)S(1)} async-done(((f32[4,48,384]{2,1,0:T(8,128)}), f32[4,48,384]{2,1,0:T(8,128)S(1)}, u32[]{:S(2)}, u32[]{:S(2)}) %all-to-all-start.2) | async-done | bytes 294944 | tf_op jit(solution)/shard_map/all_to_all | solution.py:255
  140.5 0.7 finish.1
  (14 shorter events, 0.4 us)
Async XLA Ops:
  3.3 38.0 %copy-start = (bf16[1,192,768]{2,1,0:T(8,128)(2,1)S(1)}, bf16[1,192,768]{2,1,0:T(8,128)(2,1)}, u32[]{:S(2)}) copy-start(bf16[1,192,768]{2,1,0:T(8,128)(2,1)} %param.4) | copy-start | bytes 884740
  3.3 37.9 %copy-start.1 = (bf16[1,192,768]{2,1,0:T(8,128)(2,1)S(1)}, bf16[1,192,768]{2,1,0:T(8,128)(2,1)}, u32[]{:S(2)}) copy-start(bf16[1,192,768]{2,1,0:T(8,128)(2,1)} %param.5) | copy-start | bytes 884740
  29.9 11.9 %collective-permute-start = (bf16[1536,384]{1,0:T(8,128)(2,1)S(1)}, bf16[1536,384]{1,0:T(8,128)(2,1)S(1)}, u32[]{:S(2)}, u32[]{:S(2)}) collective-permute-start(bf16[1536,384]{1,0:T(8,128)(2,1)S(1)} %bitcast.11), channel_id=1, source_target_pairs={{0,64},{64,0},{1,65},{65,1},{2,66},{66,2},{3,67},{67,3},{4,68},{68... | collective-permute-start | bytes 3538952 | tf_op jit(solution)/shard_map/ppermute | solution.py:203
  31.8 5.3 %collective-permute-start.1 = (bf16[96,768]{1,0:T(8,128)(2,1)S(1)}, bf16[96,768]{1,0:T(8,128)(2,1)S(1)}, u32[]{:S(2)}, u32[]{:S(2)}) collective-permute-start(bf16[96,768]{1,0:T(8,128)(2,1)S(1)} %get-tuple-element.16), channel_id=1, source_target_pairs={{0,1},{1,2},{2,3},{3,4},{4,5},{5,6},{6,7},{7,8},{8,9},{9,10},{10,1... | collective-permute-start | bytes 442376 | tf_op jit(solution)/shard_map/ppermute | solution.py:201
  33.1 8.1 %collective-permute-start.2 = (bf16[96,768]{1,0:T(8,128)(2,1)S(1)}, bf16[96,768]{1,0:T(8,128)(2,1)S(1)}, u32[]{:S(2)}, u32[]{:S(2)}) collective-permute-start(bf16[96,768]{1,0:T(8,128)(2,1)S(1)} %get-tuple-element.17), channel_id=1, source_target_pairs={{1,0},{2,1},{3,2},{4,3},{5,4},{6,5},{7,6},{8,7},{9,8},{10,9},{11,1... | collective-permute-start | bytes 442376 | tf_op jit(solution)/shard_map/ppermute | solution.py:200
  41.8 1.0 copy-start.2
  42.8 1.3 copy-start.3
  46.9 1.0 copy-start.4
  47.9 0.7 copy-start.6
  48.6 4.7 %collective-permute-start.3 = (bf16[8,192,384]{2,1,0:T(8,128)(2,1)S(1)}, bf16[8,192,384]{2,1,0:T(8,128)(2,1)S(1)}, u32[]{:S(2)}, u32[]{:S(2)}) collective-permute-start(bf16[8,192,384]{2,1,0:T(8,128)(2,1)S(1)} %get-tuple-element.24), channel_id=1, source_target_pairs={{0,64},{64,0},{1,65},{65,1},{2,66},{66,2},{3,67},{67,3},{4,68},{68... | collective-permute-start | bytes 3538952 | tf_op jit(solution)/shard_map/ppermute | solution.py:239
  89.2 44.3 %copy-start.7 = (bf16[256,384]{1,0:T(8,128)(2,1)S(1)}, bf16[256,384]{1,0:T(8,128)(2,1)}, u32[]{:S(2)}) copy-start(bf16[256,384]{1,0:T(8,128)(2,1)} %copy-done.6) | copy-start | bytes 589828
  129.6 11.0 %all-to-all-start.2 = ((f32[4,48,384]{2,1,0:T(8,128)}), f32[4,48,384]{2,1,0:T(8,128)S(1)}, u32[]{:S(2)}, u32[]{:S(2)}) async-start(f32[4,48,384]{2,1,0:T(8,128)} %spread.1), calls=%async_computation.2 | async-start | bytes 589824 | tf_op jit(solution)/shard_map/all_to_all | solution.py:255
  133.6 1.3 copy-start.5
